TPU v7x, 512 devices: a whole 4x8x8 slice. The times are simulated.
512 devices in a mesh: seq: 64 (over z, y_lo, core), head: 8 (over y_hi, x).
Axes of the slice: x: 4, y: 8 (y_hi: 2, y_lo: 4; y = y_hi * 4 + y_lo), z: 8, core: 2. Of those that a mesh axis runs over, the one named last changes fastest.
Arguments:
- query_in: bfloat16 [24576, 2048], P('seq', 'head'), may hold values from -6 to 6
- key_in: bfloat16 [24576, 2048], P('seq', 'head'), may hold values from -6 to 6
- value_in: bfloat16 [24576, 2048], P('seq', 'head'), may hold values from -6 to 6
- text_keys: bfloat16 [256, 2048], P(None, 'head'), may hold values from -6 to 6
- text_values: bfloat16 [256, 2048], P(None, 'head'), may hold values from -6 to 6
- text_mask: int32 [256], replicated, may hold values 0 or 1
- window_reach: int32 [16, 2], P('head'), may hold values from 0 to 1
- tile_map: int32 [64, 3], replicated, may hold values from 0 to 14, as said below
- out_weight: bfloat16 [2048, 3072], P('head'), may hold values from -0.125 to 0.125
- gate_scale: float32 [3072], replicated, may hold values from -4 to 4
- grad_out: bfloat16 [24576, 3072], P('seq', 'head'), may hold values from -12 to 12
Outputs:
- grad_query: bfloat16 [24576, 2048], P('seq', 'head')
- grad_key: bfloat16 [24576, 2048], P('seq', 'head')
- grad_value: bfloat16 [24576, 2048], P('seq', 'head')
- grad_text_keys: bfloat16 [256, 2048], P(None, 'head')
- grad_text_values: bfloat16 [256, 2048], P(None, 'head')
- grad_gate: float32 [3072], replicated
Inputs may be any that keep to these rules, and one draw needn't show every extreme that they name: `tile_map`: index i of seq sits at grid row i // 8 and grid column i % 8. Its tile row is that grid row, or 7 minus it, plus an offset; its tile column is the grid column, or 7 minus it, plus an offset; the mirroring and the offsets are the same for all indices, and so is the frame coordinate. Of the two offsets, the one of the longer grid dimension (rows when they are equal) is 7, the other 0.
All inputs are finite; a program needn't handle non-finite values.
Results may differ from a plain program's by a relative error of at most 0.02035.
The roundings to bfloat16 on the way count: a program that leaves them out, or rounds other values in their place, can miss the bound.
Values may be sent and summed in bfloat16 or wider, within the bound.
No kernel may reach another device: no remote copies, remote signals or barrier semaphores. Data moves between devices by JAX's collectives and lax.ppermute only.
A program may use at most 64 MiB of HBM per device.

v0:
```python
import jax
import jax.numpy as jnp
import numpy as np
from jax import lax
from jax.sharding import PartitionSpec as P

HEAD_DIM = 128
TILE_T = 6
TILE_H = 8
TILE_W = 8
COLS = 8
theta_base = 256.0


def from_behind(array, axis, by):
    length = lax.axis_size(axis)
    pairs = [(i, i + by) for i in range(length) if 0 <= i + by < length]
    return lax.ppermute(array, axis, pairs)


def sections(head_dim):
    first = head_dim // 8
    second = (head_dim - first) // 2
    return ((0, first), (first, second), (first + second, second))


def rotate(values, frame_pos, row_pos, col_pos, direction):
    pieces = []
    for (offset, length), where_pos in zip(
        sections(values.shape[-1]), (frame_pos, row_pos, col_pos)
    ):
        half_len = length // 2
        freqs = theta_base ** (-2.0 * jnp.arange(half_len, dtype=jnp.float32) / length)
        angles = where_pos.astype(jnp.float32)[:, None] * freqs[None, :]
        cosine = jnp.cos(angles)[:, None, :]
        sine_part = jnp.sin(angles)[:, None, :]
        first_half = values[..., offset : offset + half_len]
        second_half = values[..., offset + half_len : offset + length]
        pieces.append(first_half * cosine - direction * second_half * sine_part)
        pieces.append(direction * first_half * sine_part + second_half * cosine)
    return jnp.concatenate(pieces, axis=-1)


def local_positions(tile_coords):
    local_index = jnp.arange(TILE_T * TILE_H * TILE_W, dtype=jnp.int32)
    plane_size = TILE_H * TILE_W
    frame_pos = tile_coords[:, 0:1] * TILE_T + (local_index // plane_size)[None, :]
    row_pos = tile_coords[:, 1:2] * TILE_H + (local_index // TILE_W % TILE_H)[None, :]
    col_pos = tile_coords[:, 2:3] * TILE_W + (local_index % TILE_W)[None, :]
    return (frame_pos.reshape(-1), row_pos.reshape(-1), col_pos.reshape(-1))


def head_scores(queries, key_block, score_scale):
    return (
        jnp.einsum("qhd,khd->hqk", queries, key_block, preferred_element_type=jnp.float32)
        * score_scale
    )


def merge_stats(running_max, running_sum, scores):
    new_max = jnp.maximum(running_max, jnp.max(scores, axis=-1))
    new_sum = running_sum * jnp.exp(running_max - new_max) + jnp.sum(
        jnp.exp(scores - new_max[..., None]), axis=-1
    )
    return (new_max, new_sum)


def on_device(
    query_in,
    key_in,
    value_in,
    text_keys,
    text_values,
    text_mask,
    window_reach,
    tile_map,
    out_weight,
    gate_scale,
    grad_out,
):
    tile_rows = query_in.shape[0]
    feature_width = query_in.shape[1]
    head_count = feature_width // HEAD_DIM
    text_count = text_keys.shape[0]
    row_count = lax.axis_size("seq") // COLS
    device = lax.axis_index("seq")
    score_scale = HEAD_DIM ** (-0.5)
    split_shape = (tile_rows, head_count, HEAD_DIM)
    own_coords = tile_map[device]
    frame_pos, row_pos, col_pos = local_positions(own_coords[None, :])
    queries = rotate(
        query_in.astype(jnp.float32).reshape(split_shape), frame_pos, row_pos, col_pos, 1.0
    ).astype(jnp.bfloat16)
    keys_rot = rotate(
        key_in.astype(jnp.float32).reshape(split_shape), frame_pos, row_pos, col_pos, 1.0
    ).astype(jnp.bfloat16)
    packed = jnp.stack([keys_rot.reshape(tile_rows, feature_width), value_in])
    row_steps = np.array([-1, -1, -1, 0, 0, 0, 1, 1, 1], dtype=np.int32)
    col_steps = np.array([-1, 0, 1, -1, 0, 1, -1, 0, 1], dtype=np.int32)
    fetched = []
    for number in range(9):
        if number == 4:
            fetched.append(packed)
        else:
            fetched.append(
                from_behind(packed, "seq", int(row_steps[number]) * COLS + int(col_steps[number]))
            )
    blocks = jnp.stack(fetched)
    source_row = device // COLS - jnp.asarray(row_steps)
    source_col = device % COLS - jnp.asarray(col_steps)
    usable_block = (
        (source_row >= 0) & (source_row < row_count) & (source_col >= 0) & (source_col < COLS)
    )
    source = jnp.clip(source_row, 0, row_count - 1) * COLS + jnp.clip(source_col, 0, COLS - 1)
    near_coords = tile_map[source]
    row_gap = jnp.abs(near_coords[:, 1] - own_coords[1])
    col_gap = jnp.abs(near_coords[:, 2] - own_coords[2])
    allowed = (
        usable_block[None, :]
        & (row_gap[None, :] <= window_reach[:, 0:1])
        & (col_gap[None, :] <= window_reach[:, 1:2])
    )
    allow_rows = allowed.T
    text_open = (text_mask == 1)[None, None, :]
    block_keys = blocks[:, 0].reshape(9, tile_rows, head_count, HEAD_DIM)
    block_values = blocks[:, 1].reshape(9, tile_rows, head_count, HEAD_DIM)
    text_key_split = text_keys.reshape(text_count, head_count, HEAD_DIM)
    text_value_split = text_values.reshape(text_count, head_count, HEAD_DIM)

    def stats_step(carry, inputs):
        key_block, allow = inputs
        scores = jnp.where(
            allow[:, None, None], head_scores(queries, key_block, score_scale), -jnp.inf
        )
        return (merge_stats(carry[0], carry[1], scores), None)

    start_stats = (
        jnp.full((head_count, tile_rows), -1e30, jnp.float32),
        jnp.zeros((head_count, tile_rows), jnp.float32),
    )
    (running_max, running_sum), _ = lax.scan(stats_step, start_stats, (block_keys, allow_rows))
    text_scores = jnp.where(text_open, head_scores(queries, text_key_split, score_scale), -jnp.inf)
    running_max, running_sum = merge_stats(running_max, running_sum, text_scores)
    log_norm = running_max + jnp.log(running_sum)

    def weights_for(key_block, allow_mask):
        scores = head_scores(queries, key_block, score_scale)
        return jnp.where(allow_mask, jnp.exp(scores - log_norm[:, :, None]), 0.0)

    def output_step(total_out, inputs):
        key_block, value_block, allow = inputs
        probs = weights_for(key_block, allow[:, None, None]).astype(jnp.bfloat16)
        return (
            total_out
            + jnp.einsum("hqk,khd->hqd", probs, value_block, preferred_element_type=jnp.float32),
            None,
        )

    total_out, _ = lax.scan(
        output_step,
        jnp.zeros((head_count, tile_rows, HEAD_DIM), jnp.float32),
        (block_keys, block_values, allow_rows),
    )
    text_probs = weights_for(text_key_split, text_open).astype(jnp.bfloat16)
    total_out = total_out + jnp.einsum(
        "hqk,khd->hqd", text_probs, text_value_split, preferred_element_type=jnp.float32
    )
    attn = total_out.transpose(1, 0, 2).reshape(tile_rows, feature_width).astype(jnp.bfloat16)
    piece = lax.all_gather(grad_out, "head", axis=1, tiled=True)
    grad_proj = (piece.astype(jnp.float32) * gate_scale[None, :]).astype(jnp.bfloat16)
    grad_acc = lax.dot_general(
        grad_proj, out_weight, (((1,), (1,)), ((), ())), preferred_element_type=jnp.float32
    )
    projected = jnp.dot(attn, out_weight, preferred_element_type=jnp.float32)
    terms = jnp.sum(piece.astype(jnp.float32) * projected, axis=0)
    gate_terms = terms
    grad_attn, gate_terms = (grad_acc, gate_terms)
    grad_heads = grad_attn.astype(jnp.bfloat16).reshape(split_shape)
    delta = jnp.sum(
        grad_heads.astype(jnp.float32) * attn.reshape(split_shape).astype(jnp.float32), axis=-1
    ).T

    def grad_block(key_block, value_block, allow_mask):
        weights = weights_for(key_block, allow_mask)
        grad_weights = jnp.einsum(
            "qhd,khd->hqk", grad_heads, value_block, preferred_element_type=jnp.float32
        )
        grad_scores = (weights * (grad_weights - delta[:, :, None])).astype(jnp.bfloat16)
        query_part = jnp.einsum(
            "hqk,khd->hqd", grad_scores, key_block, preferred_element_type=jnp.float32
        )
        key_part = (
            jnp.einsum("hqk,qhd->khd", grad_scores, queries, preferred_element_type=jnp.float32)
            * score_scale
        )
        value_part = jnp.einsum(
            "hqk,qhd->khd",
            weights.astype(jnp.bfloat16),
            grad_heads,
            preferred_element_type=jnp.float32,
        )
        return (query_part, key_part, value_part)

    text_query_part, text_key_part, text_value_part = grad_block(
        text_key_split, text_value_split, text_open
    )
    text_key_grad = text_key_part.reshape(text_count, feature_width)
    text_value_grad = text_value_part.reshape(text_count, feature_width)

    def back_step(query_acc, inputs):
        key_block, value_block, allow = inputs
        query_part, key_part, value_part = grad_block(key_block, value_block, allow[:, None, None])
        stacked = jnp.stack(
            [
                key_part.reshape(tile_rows, feature_width),
                value_part.reshape(tile_rows, feature_width),
            ]
        )
        return (query_acc + query_part, stacked)

    query_acc, partials = lax.scan(
        back_step,
        jnp.zeros((head_count, tile_rows, HEAD_DIM), jnp.float32),
        (block_keys, block_values, allow_rows),
    )
    own_total = partials[4]
    for number in range(9):
        if number != 4:
            own_total = own_total + from_behind(
                partials[number].astype(jnp.bfloat16),
                "seq",
                -(int(row_steps[number]) * COLS + int(col_steps[number])),
            ).astype(jnp.float32)
    query_acc = query_acc + text_query_part
    text_key_sum, text_value_sum = lax.psum((text_key_grad, text_value_grad), "seq")
    grad_gate = lax.psum(gate_terms, ("seq", "head"))
    grad_query = (
        rotate((query_acc * score_scale).transpose(1, 0, 2), frame_pos, row_pos, col_pos, -1.0)
        .astype(jnp.bfloat16)
        .reshape(tile_rows, feature_width)
    )
    grad_key = (
        rotate(own_total[0].reshape(split_shape), frame_pos, row_pos, col_pos, -1.0)
        .astype(jnp.bfloat16)
        .reshape(tile_rows, feature_width)
    )
    grad_value = own_total[1].astype(jnp.bfloat16)
    return (
        grad_query,
        grad_key,
        grad_value,
        text_key_sum.astype(jnp.bfloat16),
        text_value_sum.astype(jnp.bfloat16),
        grad_gate,
    )


def solution(mesh):
    placed = (
        P("seq", "head"),
        P("seq", "head"),
        P("seq", "head"),
        P(None, "head"),
        P(None, "head"),
        P(),
        P("head", None),
        P(),
        P("head", None),
        P(),
        P("seq", "head"),
    )
    return jax.shard_map(
        on_device,
        mesh=mesh,
        in_specs=placed,
        out_specs=(
            P("seq", "head"),
            P("seq", "head"),
            P("seq", "head"),
            P(None, "head"),
            P(None, "head"),
            P(),
        ),
        check_vma=False,
    )
```

profile of v0, /device:TPU:2, one launch (start us, length us, event | category | flops | bytes accessed | tf_op | source)
XLA Modules:
  0.0 668.5 jit_solution(16040238661851726279)
XLA Ops:
  18.0 1.8 copy.175
  25.4 1.7 copy.171
  27.2 2.4 broadcast_multiply_fusion
  29.5 2.1 add_convert_fusion.8
  32.2 2.1 concatenate.16
  36.2 5.0 collective-permute-start.6
  41.2 5.4 collective-permute-start.5
  46.7 2.0 collective-permute-start.4
  50.0 1.3 collective-permute-start
  55.3 1.7 copy.182
  57.0 1.5 copy.135
  58.5 1.4 concatenate.17
  60.1 1.4 gather_fusion
  61.6 1.8 select_reduce_fusion
  63.4 1.3 fusion.73
  66.2 3.7 collective-permute-done
  72.2 1.3 collective-permute-start.3
  74.5 15.0 %collective-permute-done.2 = bf16[2,384,256]{1,2,0:T(8,128)(2,1)S(1)} collective-permute-done((bf16[2,384,256]{1,2,0:T(8,128)(2,1)}, bf16[2,384,256]{1,2,0:T(8,128)(2,1)S(1)}, u32[]{:S(2)}, u32[]{:S(2)}) %collective-permute-start.2) | collective-permute-done | bytes 393248 | tf_op jit(solution)/shard_map/ppermute | solution.py:18
  89.5 1.5 collective-permute-start.7
  94.5 1.9 collective-permute-done.7
  96.5 2.3 fusion.93
  98.8 3.8 copy.126
  102.6 13.8 %while.37 = (s32[]{:T(128)}, f32[2,384]{1,0:T(2,128)S(1)}, f32[2,384]{1,0:T(2,128)S(1)}, pred[9,2]{1,0:T(8,128)(4,1)S(1)}, bf16[9,384,2,128]{3,1,2,0:T(8,128)(2,...) while((s32[]{:T(128)}, f32[2,384]{1,0:T(2,128)S(1)}, f32[2,384]{1,0:T(2,128)S(1)}, ...), condition=%wide.region_3.4_spmd.clone, body=%wide.region_0.3_spmd.clone.sunk | while | flops 76975872 | bytes 2792566 | solution.py:141
  117.0 3.9 copy.128
  121.2 29.6 %while.38 = (s32[]{:T(128)}, f32[2,384,128]{2,1,0:T(8,128)}, pred[9,2]{1,0:T(8,128)(4,1)}, bf16[9,384,2,128]{3,1,2,0:T(8,128)(2,1)}, bf16[384,2,128]{2,0,1:T(8,1...) while((s32[]{:T(128)}, f32[2,384,128]{2,1,0:T(8,128)}, ...), condition=%wide.region_7.8_spmd.clone, body=%wide.region_6.7_spmd.clone.sunk | while | flops 152371200 | bytes 1380984 | solution.py:159
  121.9 2.4 fusion.151
  125.0 2.6 fusion.151
  128.3 2.6 fusion.151
  131.6 2.6 fusion.151
  134.9 2.6 fusion.151
  138.2 2.6 fusion.151
  141.5 2.6 fusion.151
  144.8 2.6 fusion.151
  148.1 2.6 fusion.151
  150.8 1.9 copy.125
  152.7 2.7 fusion.53
  158.5 55.7 %while.39 = (s32[]{:T(128)}, f32[2,384,128]{2,1,0:T(8,128)S(1)}, f32[9,2,384,256]{2,3,1,0:T(8,128)}, pred[9,2]{1,0:T(8,128)(4,1)}, bf16[9,384,2,128]{3,1,2,0:T(8...) while((s32[]{:T(128)}, f32[2,384,128]{2,1,0:T(8,128)S(1)}, ...), condition=%wide.region_10.11_spmd.clone, body=%wide.region_9.10_spmd.clone.sunk | while | flops 380043264 | bytes 9836705 | solution.py:221
  162.0 1.4 convolution_add_fusion.4
  168.2 1.4 convolution_add_fusion.4
  174.4 1.4 convolution_add_fusion.4
  180.6 1.4 convolution_add_fusion.4
  186.8 1.4 convolution_add_fusion.4
  193.0 1.4 convolution_add_fusion.4
  196.3 1.3 fusion.162
  199.1 1.4 convolution_add_fusion.4
  202.5 1.3 fusion.162
  205.3 1.4 convolution_add_fusion.4
  211.5 1.4 convolution_add_fusion.4
  214.2 3.6 convert.109
  217.7 1.8 slice_bitcast_fusion.7
  219.5 5.7 collective-permute-start.8
  226.5 1.3 collective-permute-start.14
  229.9 1.8 copy.146
  233.0 1.3 collective-permute-start.12
  234.3 2.5 fusion.45
  236.9 126.0 %psum.23 = f32[3072]{0:T(1024)} all-reduce(f32[3072]{0:T(1024)S(1)} %fusion.45), channel_id=1, replica_groups=mesh['seq'=64,'head'=8] {'seq','head'}, use_global_device_ids=true, to_apply=%region_14.15 | all-reduce | flops 3072 | bytes 24576 | tf_op jit(solution)/shard_map/psum | solution.py:236
  362.9 2.5 collective-permute-start.11
  365.4 7.6 %collective-permute-start.10 = (bf16[2,384,256]{1,2,0:T(8,128)(2,1)}, bf16[2,384,256]{1,2,0:T(8,128)(2,1)}, u32[]{:S(2)}, u32[]{:S(2)}) collective-permute-start(bf16[2,384,256]{1,2,0:T(8,128)(2,1)} %get-tuple-element.347), channel_id=1, source_target_pairs={{0,56},{8,64},{16,72},{24,80},{32,88},{40,96},{48,104},{56,112},{6... | collective-permute-start | bytes 1179656 | tf_op jit(solution)/shard_map/ppermute | solution.py:18
  373.0 2.4 collective-permute-start.9
  375.7 269.2 %all-reduce.2 = (bf16[256,256]{1,0:T(8,128)(2,1)}, bf16[256,256]{1,0:T(8,128)(2,1)}) all-reduce(f32[256,256]{1,0:T(8,128)} %copy.146, f32[256,256]{1,0:T(8,128)S(1)} %copy.148), channel_id=1, replica_groups=mesh['seq'=64,'head'=8] {'seq'}, use_global_device_ids=true, to_apply=%region_11.12 | all-reduce | flops 131072 | bytes 786432 | tf_op jit(solution)/shard_map/psum | solution.py:235
  644.9 2.5 fusion.63
  653.8 2.2 add_convert_fusion.2
  656.1 1.3 add_convert_fusion
  657.4 1.6 concatenate.18
  (280 shorter events, 108.7 us)
Async XLA Ops:
  7.2 145.5 %copy-start = (bf16[256,3072]{1,0:T(8,128)(2,1)S(1)}, bf16[256,3072]{1,0:T(8,128)(2,1)}, u32[]{:S(2)}) copy-start(bf16[256,3072]{1,0:T(8,128)(2,1)} %param.27) | copy-start | bytes 4718596
  7.2 4.3 copy-start.31
  7.2 7.7 %copy-start.28 = (bf16[384,256]{1,0:T(8,128)(2,1)S(1)}, bf16[384,256]{1,0:T(8,128)(2,1)}, u32[]{:S(2)}) copy-start(bf16[384,256]{1,0:T(8,128)(2,1)} %param.21) | copy-start | bytes 589828
  7.2 145.5 %all-gather.2.cloned.1.call-start = ((), (), s32[]{:S(2)}) async-start(), calls=%async_computation | async-start | bytes 2654208 | tf_op jit(solution)/shard_map/all_gather | solution.py:169
  14.8 14.8 %copy-start.6 = (f32[384,8]{1,0:T(8,128)}, f32[384,8]{1,0:T(8,128)S(1)}, u32[]{:S(2)}) copy-start(f32[384,8]{1,0:T(8,128)S(1)} %copy.103) | copy-start | bytes 36868
  27.1 4.5 copy-start.9
  27.1 4.5 copy-start.10
  27.1 4.5 copy-start.11
  27.1 4.5 copy-start.12
  27.1 4.5 copy-start.13
  27.1 4.5 copy-start.14
  27.1 4.5 copy-start.15
  27.1 4.5 copy-start.16
  29.5 2.7 copy-start.2
  32.2 21.0 %copy-start.32 = (s32[2,2]{1,0:T(2,128)S(1)}, s32[2,2]{1,0:T(2,128)}, u32[]{:S(2)}) copy-start(s32[2,2]{1,0:T(2,128)} %param.25) | copy-start | bytes 52
  35.4 23.1 %copy-start.4 = (bf16[384,2,128]{0,2,1:T(8,128)(2,1)}, bf16[384,2,128]{0,2,1:T(8,128)(2,1)S(1)}, u32[]{:S(2)}) copy-start(bf16[384,2,128]{0,2,1:T(8,128)(2,1)S(1)} %copy.110) | copy-start | bytes 589828
  36.2 57.2 %collective-permute-start.6 = (bf16[2,384,256]{1,2,0:T(8,128)(2,1)}, bf16[2,384,256]{1,2,0:T(8,128)(2,1)}, u32[]{:S(2)}, u32[]{:S(2)}) collective-permute-start(bf16[2,384,256]{1,2,0:T(8,128)(2,1)} %pad_maximum_fusion), channel_id=1, source_target_pairs={{0,64},{8,72},{16,80},{24,88},{32,96},{40,104},{48,112},{56,120},{... | collective-permute-start | bytes 1179656 | tf_op jit(solution)/shard_map/ppermute | solution.py:18
  41.2 51.1 %collective-permute-start.5 = (bf16[2,384,256]{1,2,0:T(8,128)(2,1)}, bf16[2,384,256]{1,2,0:T(8,128)(2,1)}, u32[]{:S(2)}, u32[]{:S(2)}) collective-permute-start(bf16[2,384,256]{1,2,0:T(8,128)(2,1)} %pad_maximum_fusion), channel_id=1, source_target_pairs={{0,56},{8,64},{16,72},{24,80},{32,88},{40,96},{48,104},{56,112},{6... | collective-permute-start | bytes 1179656 | tf_op jit(solution)/shard_map/ppermute | solution.py:18
  46.7 44.6 %collective-permute-start.4 = (bf16[2,384,256]{1,2,0:T(8,128)(2,1)}, bf16[2,384,256]{1,2,0:T(8,128)(2,1)}, u32[]{:S(2)}, u32[]{:S(2)}) collective-permute-start(bf16[2,384,256]{1,2,0:T(8,128)(2,1)} %pad_maximum_fusion), channel_id=1, source_target_pairs={{0,8},{8,16},{16,24},{24,32},{32,40},{40,48},{48,56},{56,64},{64,7... | collective-permute-start | bytes 1179656 | tf_op jit(solution)/shard_map/ppermute | solution.py:18
  48.7 23.5 %collective-permute-start.1 = (bf16[2,384,256]{1,2,0:T(8,128)(2,1)}, bf16[2,384,256]{1,2,0:T(8,128)(2,1)}, u32[]{:S(2)}, u32[]{:S(2)}) collective-permute-start(bf16[2,384,256]{1,2,0:T(8,128)(2,1)} %pad_maximum_fusion), channel_id=1, source_target_pairs={{64,0},{72,8},{80,16},{88,24},{96,32},{104,40},{112,48},{120,56},{... | collective-permute-start | bytes 1179656 | tf_op jit(solution)/shard_map/ppermute | solution.py:18
  50.0 19.8 %collective-permute-start = (bf16[2,384,256]{1,2,0:T(8,128)(2,1)}, bf16[2,384,256]{1,2,0:T(8,128)(2,1)}, u32[]{:S(2)}, u32[]{:S(2)}) collective-permute-start(bf16[2,384,256]{1,2,0:T(8,128)(2,1)} %pad_maximum_fusion), channel_id=1, source_target_pairs={{72,0},{80,8},{88,16},{96,24},{104,32},{112,40},{120,48},{128,56},... | collective-permute-start | bytes 1179656 | tf_op jit(solution)/shard_map/ppermute | solution.py:18
  63.4 27.8 %copy-start.5 = (bf16[384,2,128]{0,2,1:T(8,128)(2,1)S(1)}, bf16[384,2,128]{0,2,1:T(8,128)(2,1)}, u32[]{:S(2)}) copy-start(bf16[384,2,128]{0,2,1:T(8,128)(2,1)} %copy-done.4) | copy-start | bytes 589828
  69.8 19.7 %collective-permute-start.2 = (bf16[2,384,256]{1,2,0:T(8,128)(2,1)}, bf16[2,384,256]{1,2,0:T(8,128)(2,1)S(1)}, u32[]{:S(2)}, u32[]{:S(2)}) collective-permute-start(bf16[2,384,256]{1,2,0:T(8,128)(2,1)} %pad_maximum_fusion), channel_id=1, source_target_pairs={{56,0},{64,8},{72,16},{80,24},{88,32},{96,40},{104,48},{112,56},{1... | collective-permute-start | bytes 1179656 | tf_op jit(solution)/shard_map/ppermute | solution.py:18
  72.2 19.0 %collective-permute-start.3 = (bf16[2,384,256]{1,2,0:T(8,128)(2,1)}, bf16[2,384,256]{1,2,0:T(8,128)(2,1)S(1)}, u32[]{:S(2)}, u32[]{:S(2)}) collective-permute-start(bf16[2,384,256]{1,2,0:T(8,128)(2,1)} %pad_maximum_fusion), channel_id=1, source_target_pairs={{8,0},{16,8},{24,16},{32,24},{40,32},{48,40},{56,48},{64,56},{72,6... | collective-permute-start | bytes 1179656 | tf_op jit(solution)/shard_map/ppermute | solution.py:18
  89.5 6.9 %collective-permute-start.7 = (bf16[2,384,256]{1,2,0:T(8,128)(2,1)}, bf16[2,384,256]{1,2,0:T(8,128)(2,1)S(1)}, u32[]{:S(2)}, u32[]{:S(2)}) collective-permute-start(bf16[2,384,256]{1,2,0:T(8,128)(2,1)} %pad_maximum_fusion), channel_id=1, source_target_pairs={{0,72},{8,80},{16,88},{24,96},{32,104},{40,112},{48,120},{56,128},... | collective-permute-start | bytes 1179656 | tf_op jit(solution)/shard_map/ppermute | solution.py:18
  116.4 0.6 copy-start.33
  117.0 3.9 copy-start.30
  117.0 3.9 copy-start.29
  152.7 3.8 copy-start.8
  152.7 3.8 copy-start.26
  217.7 10.1 %copy-start.1 = (bf16[2,384,256]{1,2,0:T(8,128)(2,1)S(1)}, bf16[2,384,256]{1,2,0:T(8,128)(2,1)}, u32[]{:S(2)}) copy-start(bf16[2,384,256]{1,2,0:T(8,128)(2,1)} %fusion.50) | copy-start | bytes 1179652
  219.5 14.8 %copy-start.27 = (bf16[2,384,128]{1,2,0:T(8,128)(2,1)S(1)}, bf16[2,384,128]{1,2,0:T(8,128)(2,1)}, u32[]{:S(2)}) copy-start(bf16[2,384,128]{1,2,0:T(8,128)(2,1)} %get-tuple-element.425) | copy-start | bytes 589828
  219.5 143.4 %collective-permute-start.8 = (bf16[2,384,256]{1,2,0:T(8,128)(2,1)}, bf16[2,384,256]{1,2,0:T(8,128)(2,1)}, u32[]{:S(2)}, u32[]{:S(2)}) collective-permute-start(bf16[2,384,256]{1,2,0:T(8,128)(2,1)} %get-tuple-element.341), channel_id=1, source_target_pairs={{0,72},{8,80},{16,88},{24,96},{32,104},{40,112},{48,120},{56,128},... | collective-permute-start | bytes 1179656 | tf_op jit(solution)/shard_map/ppermute | solution.py:18
  225.3 140.1 %collective-permute-start.15 = (bf16[2,384,256]{1,2,0:T(8,128)(2,1)}, bf16[2,384,256]{1,2,0:T(8,128)(2,1)}, u32[]{:S(2)}, u32[]{:S(2)}) collective-permute-start(bf16[2,384,256]{1,2,0:T(8,128)(2,1)} %get-tuple-element.342), channel_id=1, source_target_pairs={{72,0},{80,8},{88,16},{96,24},{104,32},{112,40},{120,48},{128,56},... | collective-permute-start | bytes 1179656 | tf_op jit(solution)/shard_map/ppermute | solution.py:18
  226.5 146.4 %collective-permute-start.14 = (bf16[2,384,256]{1,2,0:T(8,128)(2,1)}, bf16[2,384,256]{1,2,0:T(8,128)(2,1)}, u32[]{:S(2)}, u32[]{:S(2)}) collective-permute-start(bf16[2,384,256]{1,2,0:T(8,128)(2,1)} %get-tuple-element.343), channel_id=1, source_target_pairs={{64,0},{72,8},{80,16},{88,24},{96,32},{104,40},{112,48},{120,56},{... | collective-permute-start | bytes 1179656 | tf_op jit(solution)/shard_map/ppermute | solution.py:18
  231.7 413.2 %collective-permute-start.13 = (bf16[2,384,256]{1,2,0:T(8,128)(2,1)}, bf16[2,384,256]{1,2,0:T(8,128)(2,1)}, u32[]{:S(2)}, u32[]{:S(2)}) collective-permute-start(bf16[2,384,256]{1,2,0:T(8,128)(2,1)} %get-tuple-element.344), channel_id=1, source_target_pairs={{56,0},{64,8},{72,16},{80,24},{88,32},{96,40},{104,48},{112,56},{1... | collective-permute-start | bytes 1179656 | tf_op jit(solution)/shard_map/ppermute | solution.py:18
  233.0 411.9 %collective-permute-start.12 = (bf16[2,384,256]{1,2,0:T(8,128)(2,1)}, bf16[2,384,256]{1,2,0:T(8,128)(2,1)}, u32[]{:S(2)}, u32[]{:S(2)}) collective-permute-start(bf16[2,384,256]{1,2,0:T(8,128)(2,1)} %get-tuple-element.345), channel_id=1, source_target_pairs={{8,0},{16,8},{24,16},{32,24},{40,32},{48,40},{56,48},{64,56},{72,6... | collective-permute-start | bytes 1179656 | tf_op jit(solution)/shard_map/ppermute | solution.py:18
  234.3 141.0 %copy-start.21 = (bf16[256,256]{0,1:T(8,128)(2,1)S(1)}, bf16[256,256]{0,1:T(8,128)(2,1)}, u32[]{:S(2)}) copy-start(bf16[256,256]{0,1:T(8,128)(2,1)} %copy.182) | copy-start | bytes 393220
  362.9 282.0 %collective-permute-start.11 = (bf16[2,384,256]{1,2,0:T(8,128)(2,1)}, bf16[2,384,256]{1,2,0:T(8,128)(2,1)}, u32[]{:S(2)}, u32[]{:S(2)}) collective-permute-start(bf16[2,384,256]{1,2,0:T(8,128)(2,1)} %get-tuple-element.346), channel_id=1, source_target_pairs={{0,8},{8,16},{16,24},{24,32},{32,40},{40,48},{48,56},{56,64},{64,7... | collective-permute-start | bytes 1179656 | tf_op jit(solution)/shard_map/ppermute | solution.py:18
  365.4 279.6 %collective-permute-start.10 = (bf16[2,384,256]{1,2,0:T(8,128)(2,1)}, bf16[2,384,256]{1,2,0:T(8,128)(2,1)}, u32[]{:S(2)}, u32[]{:S(2)}) collective-permute-start(bf16[2,384,256]{1,2,0:T(8,128)(2,1)} %get-tuple-element.347), channel_id=1, source_target_pairs={{0,56},{8,64},{16,72},{24,80},{32,88},{40,96},{48,104},{56,112},{6... | collective-permute-start | bytes 1179656 | tf_op jit(solution)/shard_map/ppermute | solution.py:18
  373.0 272.0 %collective-permute-start.9 = (bf16[2,384,256]{1,2,0:T(8,128)(2,1)}, bf16[2,384,256]{1,2,0:T(8,128)(2,1)}, u32[]{:S(2)}, u32[]{:S(2)}) collective-permute-start(bf16[2,384,256]{1,2,0:T(8,128)(2,1)} %get-tuple-element.348), channel_id=1, source_target_pairs={{0,64},{8,72},{16,80},{24,88},{32,96},{40,104},{48,112},{56,120},{... | collective-permute-start | bytes 1179656 | tf_op jit(solution)/shard_map/ppermute | solution.py:18
  648.2 5.6 copy-start.7
  652.0 4.1 copy-start.3
  652.0 4.1 copy-start.22
  653.8 2.2 copy-start.17
  653.8 2.2 copy-start.18
  653.8 2.2 copy-start.19
  653.8 2.2 copy-start.20
  653.8 2.2 copy-start.23
  657.4 2.6 copy-start.24
  657.4 2.6 copy-start.25
Sparse Core Ops, SparseCore 0:
  51.4 93.9 all-gather.1
where the time goes:
time: 672 us; the launch traced here: 668 us
  blocking collectives  395 us (59%)
  matrix products  86.9 us (13%)
  local copies, waits for them, and re-layouts  73.9 us (11%)
  starting transfers between devices  42.5 us (6%)
  other arithmetic  32 us (5%)
  waiting for transfers between devices  20.7 us (3%)
  between operations  16.5 us (2%)
    psum x1, blocking collectives, on_device(): lax.psum((text_key_grad, text_value_grad), 'seq')  269 us
    psum x1, blocking collectives, on_device(): grad_gate = lax.psum(gate_terms, ('seq', 'head'))  126 us
    ppermute x16, starting transfers between devices, from_behind(): return lax.ppermute(array, axis, pairs)  42.4 us
    unnamed x103, local copies, waits for them, and re-layouts  36.4 us
    dot_general x19, matrix products, head_scores(): jnp.einsum('qhd,khd->hqk', queries, key_block, preferred_element_type=jnp...  24.8 us
    dot_general x9, matrix products, output_step(): jnp.einsum('hqk,khd->hqd', probs, value_block, preferred_element_type=jnp...  23.4 us
    ppermute x16, waiting for transfers between devices, from_behind(): return lax.ppermute(array, axis, pairs)  20.7 us
  transfers between devices with their start and end apart: 17, of which 3 were waited for; matrix products, arithmetic and copies ran while one was open for 12% of the time, Pallas kernels for 0%

commit v1 on v0

--- a/solution.py
+++ b/solution.py
@@ -233,7 +233,9 @@
             ).astype(jnp.float32)
     query_acc = query_acc + text_query_part
     text_key_sum, text_value_sum = lax.psum((text_key_grad, text_value_grad), "seq")
-    grad_gate = lax.psum(gate_terms, ("seq", "head"))
+    grad_gate = gate_terms
+    for nth in ("seq", "head"):
+        grad_gate = lax.psum(grad_gate, nth)
     grad_query = (
         rotate((query_acc * score_scale).transpose(1, 0, 2), frame_pos, row_pos, col_pos, -1.0)
         .astype(jnp.bfloat16)

time: 672 us -> 622 us (0.926)
  the two profiles are of different devices: /device:TPU:2 before, /device:TPU:256 now
where the time goes in v1:
time: 622 us; the launch traced here: 619 us
  blocking collectives  332 us (53%)
  matrix products  86.9 us (14%)
  local copies, waits for them, and re-layouts  68.3 us (11%)
  starting transfers between devices  60.9 us (10%)
  other arithmetic  33 us (5%)
  waiting for transfers between devices  20.1 us (3%)
  between operations  16.9 us (3%)
    psum x1, blocking collectives, on_device(): lax.psum((text_key_grad, text_value_grad), 'seq')  279 us
    ppermute x16, starting transfers between devices, from_behind(): return lax.ppermute(array, axis, pairs)  60.9 us
    psum x1, blocking collectives, on_device(): grad_gate = lax.psum(grad_gate, nth)  53.6 us
    unnamed x111, local copies, waits for them, and re-layouts  33.3 us
    dot_general x19, matrix products, head_scores(): jnp.einsum('qhd,khd->hqk', queries, key_block, preferred_element_type=jnp...  24.7 us
    dot_general x9, matrix products, output_step(): jnp.einsum('hqk,khd->hqd', probs, value_block, preferred_element_type=jnp...  23.3 us
    ppermute x16, waiting for transfers between devices, from_behind(): return lax.ppermute(array, axis, pairs)  20.1 us
    dot_general x10, matrix products, grad_block(): jnp.einsum('hqk,khd->hqd', grad_scores, key_block, preferred_element_type...  12.5 us
  transfers between devices with their start and end apart: 17, of which 2 were waited for; matrix products, arithmetic and copies ran while one was open for 13% of the time, Pallas kernels for 0%

profile of v1, /device:TPU:256, one launch (start us, length us, event | category | flops | bytes accessed | tf_op | source)
XLA Modules:
  0.0 619.3 jit_solution(4183919905529003316)
XLA Ops:
  25.1 2.4 broadcast_multiply_fusion
  27.5 2.1 add_convert_fusion.8
  30.9 1.5 concatenate.16
  33.4 3.4 collective-permute-start.6
  36.8 4.7 collective-permute-start.5
  41.4 1.9 collective-permute-start.4
  43.4 3.7 collective-permute-start.1
  47.0 5.8 collective-permute-start
  56.9 1.7 copy.182
  58.5 1.5 copy.135
  60.0 1.4 concatenate.17
  61.7 1.4 gather_fusion
  63.1 1.8 select_reduce_fusion
  64.9 1.5 fusion.73
  67.9 1.9 collective-permute-start.2
  70.9 5.6 collective-permute-start.3
  77.6 5.5 collective-permute-done.2
  83.1 2.1 collective-permute-start.7
  88.6 14.6 %collective-permute-done.7 = bf16[2,384,256]{1,2,0:T(8,128)(2,1)S(1)} collective-permute-done((bf16[2,384,256]{1,2,0:T(8,128)(2,1)}, bf16[2,384,256]{1,2,0:T(8,128)(2,1)S(1)}, u32[]{:S(2)}, u32[]{:S(2)}) %collective-permute-start.7) | collective-permute-done | bytes 393248 | tf_op jit(solution)/shard_map/ppermute | solution.py:18
  103.3 2.3 fusion.93
  105.6 3.8 copy.126
  109.4 13.8 %while.37 = (s32[]{:T(128)}, f32[2,384]{1,0:T(2,128)S(1)}, f32[2,384]{1,0:T(2,128)S(1)}, pred[9,2]{1,0:T(8,128)(4,1)S(1)}, bf16[9,384,2,128]{3,1,2,0:T(8,128)(2,...) while((s32[]{:T(128)}, f32[2,384]{1,0:T(2,128)S(1)}, f32[2,384]{1,0:T(2,128)S(1)}, ...), condition=%wide.region_3.4_spmd.clone, body=%wide.region_0.3_spmd.clone.sunk | while | flops 76975872 | bytes 2792566 | solution.py:141
  123.8 3.9 copy.128
  127.9 29.5 %while.38 = (s32[]{:T(128)}, f32[2,384,128]{2,1,0:T(8,128)}, pred[9,2]{1,0:T(8,128)(4,1)}, bf16[9,384,2,128]{3,1,2,0:T(8,128)(2,1)}, bf16[384,2,128]{2,0,1:T(8,1...) while((s32[]{:T(128)}, f32[2,384,128]{2,1,0:T(8,128)}, ...), condition=%wide.region_7.8_spmd.clone, body=%wide.region_6.7_spmd.clone.sunk | while | flops 152371200 | bytes 1380984 | solution.py:159
  128.6 2.4 fusion.151
  131.7 2.6 fusion.151
  135.0 2.6 fusion.151
  138.3 2.6 fusion.151
  141.6 2.6 fusion.151
  144.9 2.6 fusion.151
  148.2 2.6 fusion.151
  151.5 2.6 fusion.151
  154.8 2.6 fusion.151
  157.4 1.9 copy.125
  159.4 2.7 fusion.53
  165.2 55.7 %while.39 = (s32[]{:T(128)}, f32[2,384,128]{2,1,0:T(8,128)S(1)}, f32[9,2,384,256]{2,3,1,0:T(8,128)}, pred[9,2]{1,0:T(8,128)(4,1)}, bf16[9,384,2,128]{3,1,2,0:T(8...) while((s32[]{:T(128)}, f32[2,384,128]{2,1,0:T(8,128)S(1)}, ...), condition=%wide.region_10.11_spmd.clone, body=%wide.region_9.10_spmd.clone.sunk | while | flops 380043264 | bytes 9836705 | solution.py:221
  165.8 1.3 fusion.162
  168.7 1.4 convolution_add_fusion.4
  174.9 1.4 convolution_add_fusion.4
  181.1 1.4 convolution_add_fusion.4
  187.3 1.4 convolution_add_fusion.4
  193.4 1.4 convolution_add_fusion.4
  196.8 1.3 fusion.162
  199.6 1.4 convolution_add_fusion.4
  205.8 1.4 convolution_add_fusion.4
  212.0 1.4 convolution_add_fusion.4
  218.2 1.4 convolution_add_fusion.4
  220.8 3.6 convert.109
  224.4 1.8 slice_bitcast_fusion.7
  226.2 1.9 collective-permute-start.8
  228.1 8.4 %collective-permute-start.15 = (bf16[2,384,256]{1,2,0:T(8,128)(2,1)}, bf16[2,384,256]{1,2,0:T(8,128)(2,1)}, u32[]{:S(2)}, u32[]{:S(2)}) collective-permute-start(bf16[2,384,256]{1,2,0:T(8,128)(2,1)} %get-tuple-element.343), channel_id=1, source_target_pairs={{72,0},{80,8},{88,16},{96,24},{104,32},{112,40},{120,48},{128,56},... | collective-permute-start | bytes 1179656 | tf_op jit(solution)/shard_map/ppermute | solution.py:18
  236.6 1.9 collective-permute-start.14
  240.7 1.9 collective-permute-start.13
  242.7 3.8 collective-permute-start.12
  246.5 2.6 fusion.45
  249.2 1.9 collective-permute-start.11
  251.1 7.9 %collective-permute-start.10 = (bf16[2,384,256]{1,2,0:T(8,128)(2,1)}, bf16[2,384,256]{1,2,0:T(8,128)(2,1)}, u32[]{:S(2)}, u32[]{:S(2)}) collective-permute-start(bf16[2,384,256]{1,2,0:T(8,128)(2,1)} %get-tuple-element.348), channel_id=1, source_target_pairs={{0,56},{8,64},{16,72},{24,80},{32,88},{40,96},{48,104},{56,112},{6... | collective-permute-start | bytes 1179656 | tf_op jit(solution)/shard_map/ppermute | solution.py:18
  259.1 3.9 collective-permute-start.9
  263.0 278.8 %all-reduce.2 = (bf16[256,256]{1,0:T(8,128)(2,1)}, bf16[256,256]{1,0:T(8,128)(2,1)}, f32[3072]{0:T(1024)S(1)}) all-reduce(f32[256,256]{1,0:T(8,128)S(1)} %copy.146, f32[256,256]{1,0:T(8,128)S(1)} %copy.148, f32[3072]{0:T(1024)S(1)} %fusion.45), channel_id=1, replica_groups=mesh['seq'=64,'head'=8] {'seq'}, use_global_device_ids=true, to_apply=%region_11.12 | all-reduce | flops 134144 | bytes 811008 | tf_op jit(solution)/shard_map/psum | solution.py:235
  541.8 53.6 %psum.31 = f32[3072]{0:T(1024)} all-reduce(f32[3072]{0:T(1024)S(1)} %get-tuple-element.339), channel_id=1, replica_groups=mesh['seq'=64,'head'=8] {'head'}, use_global_device_ids=true, to_apply=%region_15.16 | all-reduce | flops 3072 | bytes 24576 | tf_op jit(solution)/shard_map/psum | solution.py:238
  595.8 2.5 fusion.63
  604.7 2.2 add_convert_fusion.2
  606.9 1.3 add_convert_fusion
  608.3 1.6 concatenate.18
  (288 shorter events, 104.6 us)
Async XLA Ops:
  7.2 152.2 %copy-start = (bf16[256,3072]{1,0:T(8,128)(2,1)S(1)}, bf16[256,3072]{1,0:T(8,128)(2,1)}, u32[]{:S(2)}) copy-start(bf16[256,3072]{1,0:T(8,128)(2,1)} %param.27) | copy-start | bytes 4718596
  7.2 4.3 copy-start.35
  7.2 8.7 %copy-start.29 = (bf16[384,256]{1,0:T(8,128)(2,1)S(1)}, bf16[384,256]{1,0:T(8,128)(2,1)}, u32[]{:S(2)}) copy-start(bf16[384,256]{1,0:T(8,128)(2,1)} %param.21) | copy-start | bytes 589828
  7.2 152.1 %all-gather.2.cloned.1.call-start = ((), (), s32[]{:S(2)}) async-start(), calls=%async_computation | async-start | bytes 2654208 | tf_op jit(solution)/shard_map/all_gather | solution.py:169
  11.5 6.6 %copy-start.32 = (f32[384,2,8]{0,2,1:T(8,128)S(1)}, f32[384,2,8]{0,2,1:T(8,128)}, u32[]{:S(2)}) copy-start(f32[384,2,8]{0,2,1:T(8,128)} %get-tuple-element.400) | copy-start | bytes 73732
  11.5 6.8 %copy-start.28 = (f32[384,2,28]{0,2,1:T(8,128)S(1)}, f32[384,2,28]{0,2,1:T(8,128)}, u32[]{:S(2)}) copy-start(f32[384,2,28]{0,2,1:T(8,128)} %get-tuple-element.397) | copy-start | bytes 258052
  15.1 12.4 %copy-start.6 = (f32[384,8]{1,0:T(8,128)}, f32[384,8]{1,0:T(8,128)S(1)}, u32[]{:S(2)}) copy-start(f32[384,8]{1,0:T(8,128)S(1)} %copy.103) | copy-start | bytes 36868
  18.1 5.8 copy-start.30
  18.3 5.8 copy-start.31
  25.0 4.6 copy-start.9
  25.0 4.6 copy-start.10
  25.0 4.6 copy-start.11
  25.0 4.6 copy-start.12
  25.0 4.6 copy-start.13
  25.0 4.6 copy-start.14
  25.1 4.6 copy-start.15
  25.1 4.6 copy-start.16
  27.5 3.4 copy-start.2
  30.9 23.9 %copy-start.36 = (s32[2,2]{1,0:T(2,128)S(1)}, s32[2,2]{1,0:T(2,128)}, u32[]{:S(2)}) copy-start(s32[2,2]{1,0:T(2,128)} %param.25) | copy-start | bytes 52
  32.6 27.5 %copy-start.4 = (bf16[384,2,128]{0,2,1:T(8,128)(2,1)}, bf16[384,2,128]{0,2,1:T(8,128)(2,1)S(1)}, u32[]{:S(2)}) copy-start(bf16[384,2,128]{0,2,1:T(8,128)(2,1)S(1)} %copy.110) | copy-start | bytes 589828
  33.4 54.2 %collective-permute-start.6 = (bf16[2,384,256]{1,2,0:T(8,128)(2,1)}, bf16[2,384,256]{1,2,0:T(8,128)(2,1)}, u32[]{:S(2)}, u32[]{:S(2)}) collective-permute-start(bf16[2,384,256]{1,2,0:T(8,128)(2,1)} %pad_maximum_fusion), channel_id=1, source_target_pairs={{0,64},{8,72},{16,80},{24,88},{32,96},{40,104},{48,112},{56,120},{... | collective-permute-start | bytes 1179656 | tf_op jit(solution)/shard_map/ppermute | solution.py:18
  36.8 49.7 %collective-permute-start.5 = (bf16[2,384,256]{1,2,0:T(8,128)(2,1)}, bf16[2,384,256]{1,2,0:T(8,128)(2,1)}, u32[]{:S(2)}, u32[]{:S(2)}) collective-permute-start(bf16[2,384,256]{1,2,0:T(8,128)(2,1)} %pad_maximum_fusion), channel_id=1, source_target_pairs={{0,56},{8,64},{16,72},{24,80},{32,88},{40,96},{48,104},{56,112},{6... | collective-permute-start | bytes 1179656 | tf_op jit(solution)/shard_map/ppermute | solution.py:18
  41.4 44.0 %collective-permute-start.4 = (bf16[2,384,256]{1,2,0:T(8,128)(2,1)}, bf16[2,384,256]{1,2,0:T(8,128)(2,1)}, u32[]{:S(2)}, u32[]{:S(2)}) collective-permute-start(bf16[2,384,256]{1,2,0:T(8,128)(2,1)} %pad_maximum_fusion), channel_id=1, source_target_pairs={{0,8},{8,16},{16,24},{24,32},{32,40},{40,48},{48,56},{56,64},{64,7... | collective-permute-start | bytes 1179656 | tf_op jit(solution)/shard_map/ppermute | solution.py:18
  43.4 27.5 %collective-permute-start.1 = (bf16[2,384,256]{1,2,0:T(8,128)(2,1)}, bf16[2,384,256]{1,2,0:T(8,128)(2,1)}, u32[]{:S(2)}, u32[]{:S(2)}) collective-permute-start(bf16[2,384,256]{1,2,0:T(8,128)(2,1)} %pad_maximum_fusion), channel_id=1, source_target_pairs={{64,0},{72,8},{80,16},{88,24},{96,32},{104,40},{112,48},{120,56},{... | collective-permute-start | bytes 1179656 | tf_op jit(solution)/shard_map/ppermute | solution.py:18
  47.0 20.9 %collective-permute-start = (bf16[2,384,256]{1,2,0:T(8,128)(2,1)}, bf16[2,384,256]{1,2,0:T(8,128)(2,1)}, u32[]{:S(2)}, u32[]{:S(2)}) collective-permute-start(bf16[2,384,256]{1,2,0:T(8,128)(2,1)} %pad_maximum_fusion), channel_id=1, source_target_pairs={{72,0},{80,8},{88,16},{96,24},{104,32},{112,40},{120,48},{128,56},... | collective-permute-start | bytes 1179656 | tf_op jit(solution)/shard_map/ppermute | solution.py:18
  64.9 20.4 %copy-start.5 = (bf16[384,2,128]{0,2,1:T(8,128)(2,1)S(1)}, bf16[384,2,128]{0,2,1:T(8,128)(2,1)}, u32[]{:S(2)}) copy-start(bf16[384,2,128]{0,2,1:T(8,128)(2,1)} %copy-done.4) | copy-start | bytes 589828
  67.9 15.2 %collective-permute-start.2 = (bf16[2,384,256]{1,2,0:T(8,128)(2,1)}, bf16[2,384,256]{1,2,0:T(8,128)(2,1)S(1)}, u32[]{:S(2)}, u32[]{:S(2)}) collective-permute-start(bf16[2,384,256]{1,2,0:T(8,128)(2,1)} %pad_maximum_fusion), channel_id=1, source_target_pairs={{56,0},{64,8},{72,16},{80,24},{88,32},{96,40},{104,48},{112,56},{1... | collective-permute-start | bytes 1179656 | tf_op jit(solution)/shard_map/ppermute | solution.py:18
  70.9 14.3 %collective-permute-start.3 = (bf16[2,384,256]{1,2,0:T(8,128)(2,1)}, bf16[2,384,256]{1,2,0:T(8,128)(2,1)S(1)}, u32[]{:S(2)}, u32[]{:S(2)}) collective-permute-start(bf16[2,384,256]{1,2,0:T(8,128)(2,1)} %pad_maximum_fusion), channel_id=1, source_target_pairs={{8,0},{16,8},{24,16},{32,24},{40,32},{48,40},{56,48},{64,56},{72,6... | collective-permute-start | bytes 1179656 | tf_op jit(solution)/shard_map/ppermute | solution.py:18
  83.1 20.1 %collective-permute-start.7 = (bf16[2,384,256]{1,2,0:T(8,128)(2,1)}, bf16[2,384,256]{1,2,0:T(8,128)(2,1)S(1)}, u32[]{:S(2)}, u32[]{:S(2)}) collective-permute-start(bf16[2,384,256]{1,2,0:T(8,128)(2,1)} %pad_maximum_fusion), channel_id=1, source_target_pairs={{0,72},{8,80},{16,88},{24,96},{32,104},{40,112},{48,120},{56,128},... | collective-permute-start | bytes 1179656 | tf_op jit(solution)/shard_map/ppermute | solution.py:18
  123.2 0.6 copy-start.37
  123.8 3.9 copy-start.34
  123.8 3.9 copy-start.33
  159.4 3.8 copy-start.8
  159.4 3.8 copy-start.27
  224.4 14.1 %copy-start.1 = (bf16[2,384,256]{1,2,0:T(8,128)(2,1)S(1)}, bf16[2,384,256]{1,2,0:T(8,128)(2,1)}, u32[]{:S(2)}) copy-start(bf16[2,384,256]{1,2,0:T(8,128)(2,1)} %fusion.50) | copy-start | bytes 1179652
  224.4 15.1 %copy-start.22 = (f32[2,128,256]{2,1,0:T(8,128)S(1)}, f32[2,128,256]{2,1,0:T(8,128)}, u32[]{:S(2)}) copy-start(f32[2,128,256]{2,1,0:T(8,128)} %fusion.89) | copy-start | bytes 786436
  226.2 23.0 %collective-permute-start.8 = (bf16[2,384,256]{1,2,0:T(8,128)(2,1)}, bf16[2,384,256]{1,2,0:T(8,128)(2,1)}, u32[]{:S(2)}, u32[]{:S(2)}) collective-permute-start(bf16[2,384,256]{1,2,0:T(8,128)(2,1)} %get-tuple-element.342), channel_id=1, source_target_pairs={{0,72},{8,80},{16,88},{24,96},{32,104},{40,112},{48,120},{56,128},... | collective-permute-start | bytes 1179656 | tf_op jit(solution)/shard_map/ppermute | solution.py:18
  228.1 23.0 %collective-permute-start.15 = (bf16[2,384,256]{1,2,0:T(8,128)(2,1)}, bf16[2,384,256]{1,2,0:T(8,128)(2,1)}, u32[]{:S(2)}, u32[]{:S(2)}) collective-permute-start(bf16[2,384,256]{1,2,0:T(8,128)(2,1)} %get-tuple-element.343), channel_id=1, source_target_pairs={{72,0},{80,8},{88,16},{96,24},{104,32},{112,40},{120,48},{128,56},... | collective-permute-start | bytes 1179656 | tf_op jit(solution)/shard_map/ppermute | solution.py:18
  236.6 22.5 %collective-permute-start.14 = (bf16[2,384,256]{1,2,0:T(8,128)(2,1)}, bf16[2,384,256]{1,2,0:T(8,128)(2,1)}, u32[]{:S(2)}, u32[]{:S(2)}) collective-permute-start(bf16[2,384,256]{1,2,0:T(8,128)(2,1)} %get-tuple-element.344), channel_id=1, source_target_pairs={{64,0},{72,8},{80,16},{88,24},{96,32},{104,40},{112,48},{120,56},{... | collective-permute-start | bytes 1179656 | tf_op jit(solution)/shard_map/ppermute | solution.py:18
  240.7 355.0 %collective-permute-start.13 = (bf16[2,384,256]{1,2,0:T(8,128)(2,1)}, bf16[2,384,256]{1,2,0:T(8,128)(2,1)}, u32[]{:S(2)}, u32[]{:S(2)}) collective-permute-start(bf16[2,384,256]{1,2,0:T(8,128)(2,1)} %get-tuple-element.345), channel_id=1, source_target_pairs={{56,0},{64,8},{72,16},{80,24},{88,32},{96,40},{104,48},{112,56},{1... | collective-permute-start | bytes 1179656 | tf_op jit(solution)/shard_map/ppermute | solution.py:18
  242.7 353.1 %collective-permute-start.12 = (bf16[2,384,256]{1,2,0:T(8,128)(2,1)}, bf16[2,384,256]{1,2,0:T(8,128)(2,1)}, u32[]{:S(2)}, u32[]{:S(2)}) collective-permute-start(bf16[2,384,256]{1,2,0:T(8,128)(2,1)} %get-tuple-element.346), channel_id=1, source_target_pairs={{8,0},{16,8},{24,16},{32,24},{40,32},{48,40},{56,48},{64,56},{72,6... | collective-permute-start | bytes 1179656 | tf_op jit(solution)/shard_map/ppermute | solution.py:18
  246.5 348.9 %copy-start.21 = (bf16[256,256]{0,1:T(8,128)(2,1)S(1)}, bf16[256,256]{0,1:T(8,128)(2,1)}, u32[]{:S(2)}) copy-start(bf16[256,256]{0,1:T(8,128)(2,1)} %copy.182) | copy-start | bytes 393220
  249.2 346.6 %collective-permute-start.11 = (bf16[2,384,256]{1,2,0:T(8,128)(2,1)}, bf16[2,384,256]{1,2,0:T(8,128)(2,1)}, u32[]{:S(2)}, u32[]{:S(2)}) collective-permute-start(bf16[2,384,256]{1,2,0:T(8,128)(2,1)} %get-tuple-element.347), channel_id=1, source_target_pairs={{0,8},{8,16},{16,24},{24,32},{32,40},{40,48},{48,56},{56,64},{64,7... | collective-permute-start | bytes 1179656 | tf_op jit(solution)/shard_map/ppermute | solution.py:18
  251.1 344.7 %collective-permute-start.10 = (bf16[2,384,256]{1,2,0:T(8,128)(2,1)}, bf16[2,384,256]{1,2,0:T(8,128)(2,1)}, u32[]{:S(2)}, u32[]{:S(2)}) collective-permute-start(bf16[2,384,256]{1,2,0:T(8,128)(2,1)} %get-tuple-element.348), channel_id=1, source_target_pairs={{0,56},{8,64},{16,72},{24,80},{32,88},{40,96},{48,104},{56,112},{6... | collective-permute-start | bytes 1179656 | tf_op jit(solution)/shard_map/ppermute | solution.py:18
  259.1 336.7 %collective-permute-start.9 = (bf16[2,384,256]{1,2,0:T(8,128)(2,1)}, bf16[2,384,256]{1,2,0:T(8,128)(2,1)}, u32[]{:S(2)}, u32[]{:S(2)}) collective-permute-start(bf16[2,384,256]{1,2,0:T(8,128)(2,1)} %get-tuple-element.349), channel_id=1, source_target_pairs={{0,64},{8,72},{16,80},{24,88},{32,96},{40,104},{48,112},{56,120},{... | collective-permute-start | bytes 1179656 | tf_op jit(solution)/shard_map/ppermute | solution.py:18
  599.0 5.6 copy-start.7
  602.8 4.1 copy-start.3
  602.8 4.1 copy-start.23
  604.7 2.2 copy-start.17
  604.7 2.2 copy-start.18
  604.7 2.2 copy-start.19
  604.7 2.2 copy-start.20
  604.7 2.2 copy-start.24
  608.3 2.6 copy-start.25
  608.3 2.6 copy-start.26
Sparse Core Ops, SparseCore 0:
  53.0 86.9 all-gather.1
